TPU v7x, 32 devices: a whole 2x2x4 slice. The times are simulated.
32 devices in a mesh: region: 4 (over z), seq: 8 (over y, x, core).
Axes of the slice: x: 2, y: 2, z: 4, core: 2. Of those that a mesh axis runs over, the one named last changes fastest.
Arguments:
- queries: bfloat16 [4096, 1024], P(('region', 'seq')), may hold values from -80 to 80
- keys: bfloat16 [4096, 1024], P(('region', 'seq')), may hold values from -8 to 8
- values: bfloat16 [4096, 1024], P(('region', 'seq')), may hold values from -6 to 6
- out_grad: bfloat16 [4096, 1024], P(('region', 'seq')), may hold values from -6 to 6
- table: int32 [4, 8, 8], P('region'), may hold values from -1 to 23, as said below
- counts: int32 [4, 8], replicated, may hold values from 2 to 128
- sendlist: int32 [4, 2, 8], replicated, may hold values from 0 to 7, as said below
Outputs:
- attended: bfloat16 [4096, 1024], P(('region', 'seq'))
- query_grad: bfloat16 [4096, 1024], P(('region', 'seq'))
- key_grad: bfloat16 [4096, 1024], P(('region', 'seq'))
- value_grad: bfloat16 [4096, 1024], P(('region', 'seq'))
Inputs may be any that keep to these rules, and one draw needn't show every extreme that they name: `table`: entry 0 of a block is the block itself; entries of one block differ; -1 marks padding and only follows live entries; an entry of 8 or more names boundary slot entry - 8 of key_ext. `sendlist`: the 8 blocks of one list differ.
All inputs are finite; a program needn't handle non-finite values.
Results may differ from a plain program's by a relative error of at most 0.035.
Values may be sent and summed in bfloat16 or wider, within the bound.
A program may use at most 128 MiB of HBM per device.

v0:
```python
from functools import partial
import math
import jax
import jax.numpy as jnp
from jax import lax
from jax.sharding import PartitionSpec as P

H = 16
HD = 64
BLK = 128
NBR = 8
BND = 8


def with_halo(cells, sides, width):
    for axis, dim in sides:
        count = lax.axis_size(axis)
        head = lax.slice_in_dim(cells, 0, width, axis=dim)
        tail = lax.slice_in_dim(cells, cells.shape[dim] - width, cells.shape[dim], axis=dim)
        cells = jnp.concatenate(
            [
                lax.ppermute(tail, axis, [(i, (i + 1) % count) for i in range(count)]),
                cells,
                lax.ppermute(head, axis, [((i + 1) % count, i) for i in range(count)]),
            ],
            axis=dim,
        )
    return cells


def attend_group(carry, inputs, key_ext, value_ext, count_ext, scale):
    key_acc, value_acc = carry
    query_grp, grad_grp, table_grp, count_grp, offset_grp = inputs
    group_size, neighbours = table_grp.shape
    heads = query_grp.shape[1]
    piece_len = query_grp.shape[2]
    depth = query_grp.shape[3]
    block_len = key_ext.shape[2]
    safe_ids = jnp.maximum(table_grp, 0)
    key_rows = key_ext[:, safe_ids].reshape(heads, group_size, neighbours * block_len, depth)
    value_rows = value_ext[:, safe_ids].reshape(heads, group_size, neighbours * block_len, depth)
    positions = jnp.arange(block_len, dtype=jnp.int32)
    key_valid = (table_grp >= 0)[:, :, None] & (
        positions[None, None, :] < count_ext[safe_ids][:, :, None]
    )
    key_valid = key_valid.reshape(group_size, neighbours * block_len)
    query_pos = jnp.arange(piece_len, dtype=jnp.int32)
    query_valid = offset_grp[:, None] + query_pos[None, :] < count_grp[:, None]
    scores = (
        jnp.einsum("bhqe,hbke->bhqk", query_grp, key_rows, preferred_element_type=jnp.float32)
        * scale
    )
    scores = jnp.where(key_valid[:, None, None, :], scores, jnp.float32(-1e30))
    peak = jnp.max(scores, axis=-1, keepdims=True)
    expo = jnp.exp(scores - peak)
    prob = (expo / jnp.sum(expo, axis=-1, keepdims=True)).astype(jnp.bfloat16)
    attended = jnp.einsum("bhqk,hbke->bhqe", prob, value_rows, preferred_element_type=jnp.float32)
    attended = jnp.where(query_valid[:, None, :, None], attended, jnp.float32(0.0)).astype(
        jnp.bfloat16
    )
    grad_masked = jnp.where(query_valid[:, None, :, None], grad_grp, jnp.zeros_like(grad_grp))
    dprob = jnp.einsum(
        "bhqe,hbke->bhqk", grad_masked, value_rows, preferred_element_type=jnp.float32
    )
    delta = jnp.sum(grad_masked.astype(jnp.float32) * attended.astype(jnp.float32), axis=-1)[
        ..., None
    ]
    dscore = (prob.astype(jnp.float32) * (dprob - delta)).astype(jnp.bfloat16)
    query_grad = (
        jnp.einsum("bhqk,hbke->bhqe", dscore, key_rows, preferred_element_type=jnp.float32) * scale
    )
    query_grad = query_grad.astype(jnp.bfloat16)
    key_part = (
        jnp.einsum("bhqk,bhqe->hbke", dscore, query_grp, preferred_element_type=jnp.float32) * scale
    )
    value_part = jnp.einsum(
        "bhqk,bhqe->hbke", prob, grad_masked, preferred_element_type=jnp.float32
    )
    flat_ids = safe_ids.reshape(-1)
    key_acc = key_acc.at[:, flat_ids].add(
        key_part.reshape(heads, group_size * neighbours, block_len, depth)
    )
    value_acc = value_acc.at[:, flat_ids].add(
        value_part.reshape(heads, group_size * neighbours, block_len, depth)
    )
    return ((key_acc, value_acc), (attended, query_grad))


def body(queries, keys, values, out_grad, table, counts, sendlist):
    seq_count = lax.axis_size("seq")
    region_count = lax.axis_size("region")
    galaxies, width = queries.shape
    pair_count = seq_count // 2
    pair_heads = 2 * H // seq_count
    pair_width = pair_heads * HD
    half_rows = galaxies // 2
    region_rows = seq_count * galaxies
    block_total = region_rows // BLK
    parity = lax.axis_index("seq") % 2
    region_now = lax.axis_index("region")

    def half_slots(matrix):
        return (
            matrix.reshape(2, half_rows, pair_count, pair_width)
            .transpose(2, 0, 1, 3)
            .reshape(seq_count, half_rows, pair_width)
        )

    query_heads, grad_heads = (
        lax.all_to_all(half_slots(queries), "seq", split_axis=0, concat_axis=1, tiled=True),
        lax.all_to_all(half_slots(out_grad), "seq", split_axis=0, concat_axis=1, tiled=True),
    )

    def all_slots(matrix):
        grouped = matrix.reshape(galaxies, pair_count, pair_width).transpose(1, 0, 2)
        return jnp.repeat(grouped, 2, axis=0)

    key_heads, value_heads = (
        lax.all_to_all(all_slots(keys), "seq", split_axis=0, concat_axis=1, tiled=True),
        lax.all_to_all(all_slots(values), "seq", split_axis=0, concat_axis=1, tiled=True),
    )
    paired = jnp.stack([key_heads[0], value_heads[0]])
    head_first = paired.reshape(2, region_rows, pair_heads, HD).transpose(0, 2, 1, 3)
    head_blocks = head_first.reshape(2, pair_heads, block_total, BLK, HD)
    my_lists = sendlist[region_now]
    prev_ids = my_lists[0]
    next_ids = my_lists[1]
    rim_rows = BND * BLK
    packed_rim = rim_rows // 2
    outgoing = jnp.concatenate(
        [head_blocks[:, :, prev_ids], head_blocks[:, :, next_ids]], axis=2
    ).reshape(2, pair_heads, rim_rows, 2 * HD)
    widened = with_halo(outgoing, (("region", 2),), packed_rim)
    from_left = widened[:, :, :packed_rim].reshape(2, pair_heads, rim_rows, HD)
    from_right = widened[:, :, -packed_rim:].reshape(2, pair_heads, rim_rows, HD)
    slots = block_total + 2 * BND
    extended = jnp.concatenate([head_first, from_left, from_right], axis=2).reshape(
        2, pair_heads, slots, BLK, HD
    )
    left_region = (region_now + region_count - 1) % region_count
    right_region = (region_now + 1) % region_count
    count_ext = jnp.concatenate(
        [
            counts[region_now],
            counts[left_region][sendlist[left_region, 1]],
            counts[right_region][sendlist[right_region, 0]],
        ]
    )
    piece_rows = min(BLK, half_rows)
    per_source = half_rows // piece_rows
    piece_starts = (
        jnp.arange(seq_count, dtype=jnp.int32)[:, None] * galaxies
        + parity * half_rows
        + jnp.arange(per_source, dtype=jnp.int32)[None, :] * piece_rows
    ).reshape(-1)
    piece_blocks = piece_starts // BLK
    piece_offsets = piece_starts % BLK
    my_table = table[0][piece_blocks]
    my_counts = counts[region_now][piece_blocks]
    piece_total = seq_count * per_source
    group_width = 8
    groups = piece_total // group_width

    def scan_layout(matrix):
        return matrix.reshape(groups, group_width, piece_rows, pair_heads, HD).transpose(
            0, 1, 3, 2, 4
        )

    stepper = partial(
        attend_group,
        key_ext=extended[0],
        value_ext=extended[1],
        count_ext=count_ext,
        scale=1.0 / math.sqrt(HD),
    )
    start = (
        jnp.zeros((pair_heads, slots, BLK, HD), jnp.float32),
        jnp.zeros((pair_heads, slots, BLK, HD), jnp.float32),
    )
    carried, outputs = lax.scan(
        stepper,
        start,
        (
            scan_layout(query_heads),
            scan_layout(grad_heads),
            my_table.reshape(groups, group_width, NBR),
            my_counts.reshape(groups, group_width),
            piece_offsets.reshape(groups, group_width),
        ),
    )
    accum = jnp.stack([carried[0], carried[1]]).reshape(2, pair_heads, slots * BLK, HD)
    inner = accum[:, :, :region_rows].reshape(2, pair_heads, block_total, BLK, HD)
    rim_out = accum[:, :, region_rows:].reshape(2, pair_heads, rim_rows, 2 * HD)
    returned = with_halo(rim_out, (("region", 2),), packed_rim)
    back_left = returned[:, :, :packed_rim].reshape(2, pair_heads, BND, BLK, HD)
    back_right = returned[:, :, -packed_rim:].reshape(2, pair_heads, BND, BLK, HD)
    inner = inner.at[:, :, prev_ids].add(back_left)
    inner = inner.at[:, :, next_ids].add(back_right)
    inner = (
        inner.reshape(2, pair_heads, region_rows, HD)
        .transpose(0, 2, 1, 3)
        .reshape(2, region_rows, pair_width)
    )
    spread = lax.all_to_all(
        inner.reshape(2, seq_count, galaxies, pair_width),
        "seq",
        split_axis=1,
        concat_axis=1,
        tiled=True,
    )
    summed = spread.reshape(2, pair_count, 2, galaxies, pair_width).sum(axis=2)
    grads = summed.transpose(0, 2, 1, 3).reshape(2, galaxies, width)
    attended_heads = outputs[0].transpose(0, 1, 3, 2, 4).reshape(seq_count, half_rows, pair_width)
    qgrad_heads = outputs[1].transpose(0, 1, 3, 2, 4).reshape(seq_count, half_rows, pair_width)
    attended_back, qgrad_back = (
        lax.all_to_all(attended_heads, "seq", split_axis=0, concat_axis=0, tiled=True),
        lax.all_to_all(qgrad_heads, "seq", split_axis=0, concat_axis=0, tiled=True),
    )

    def owner_rows(received):
        return (
            received.reshape(pair_count, 2, half_rows, pair_width)
            .transpose(1, 2, 0, 3)
            .reshape(galaxies, width)
        )

    grads = grads.astype(jnp.bfloat16)
    return (owner_rows(attended_back), owner_rows(qgrad_back), grads[0], grads[1])


def solution(mesh):
    return jax.shard_map(
        body,
        mesh=mesh,
        in_specs=(
            P(("region", "seq"), None),
            P(("region", "seq"), None),
            P(("region", "seq"), None),
            P(("region", "seq"), None),
            P("region", None, None),
            P(),
            P(),
        ),
        out_specs=(
            P(("region", "seq"), None),
            P(("region", "seq"), None),
            P(("region", "seq"), None),
            P(("region", "seq"), None),
        ),
        check_vma=False,
    )
```

profile of v0, /device:TPU:0, one launch (start us, length us, event | category | flops | bytes accessed | tf_op | source)
XLA Modules:
  0.0 426.3 jit_solution(13458127873232549518)
XLA Ops:
  3.0 5.2 %all-to-all-start.1 = ((bf16[8,128,256]{1,2,0:T(8,128)(2,1)}), bf16[8,128,256]{1,2,0:T(8,128)(2,1)S(1)}, u32[]{:S(2)}, u32[]{:S(2)}) async-start(bf16[8,128,256]{1,2,0:T(8,128)(2,1)} %bitcast.15), calls=%async_computation.1 | async-start | bytes 1048576 | tf_op jit(solution)/shard_map/all_to_all | solution.py:120
  11.1 6.8 %all-to-all-done.1 = bf16[8,128,256]{1,2,0:T(8,128)(2,1)S(1)} async-done(((bf16[8,128,256]{1,2,0:T(8,128)(2,1)}), bf16[8,128,256]{1,2,0:T(8,128)(2,1)S(1)}, u32[]{:S(2)}, u32[]{:S(2)}) %all-to-all-start.1) | async-done | bytes 524320 | tf_op jit(solution)/shard_map/all_to_all | solution.py:120
  18.7 3.5 all-to-all-start
  25.1 6.8 %all-to-all-done = bf16[8,128,256]{1,2,0:T(8,128)(2,1)S(1)} async-done(((bf16[8,128,256]{1,2,0:T(8,128)(2,1)}), bf16[8,128,256]{1,2,0:T(8,128)(2,1)S(1)}, u32[]{:S(2)}, u32[]{:S(2)}) %all-to-all-start) | async-done | bytes 524320 | tf_op jit(solution)/shard_map/all_to_all | solution.py:119
  31.9 3.4 all-to-all-start.4
  40.4 4.8 %copy.175 = bf16[2,4,16,128,64]{4,3,2,1,0:T(8,128)(2,1)} copy(bf16[2,4,16,128,64]{3,4,1,0,2:T(8,128)(2,1)} %pad_maximum_fusion.1) | data formatting | bytes 4194304 | tf_op jit(solution)/shard_map/concatenate | solution.py:130
  45.2 5.0 %reshape.426 = bf16[2,4,1024,128]{3,2,1,0:T(8,128)(2,1)S(1)} reshape(bf16[2,4,16,128,64]{4,3,2,1,0:T(8,128)(2,1)} %copy.175) | data formatting | bytes 4194304 | tf_op jit(solution)/shard_map/reshape | solution.py:132
  51.7 3.6 collective-permute-start.1
  59.3 4.3 %all-to-all-start.2 = ((bf16[8,64,256]{2,1,0:T(8,128)(2,1)}), bf16[8,64,256]{2,1,0:T(8,128)(2,1)S(1)}, u32[]{:S(2)}, u32[]{:S(2)}) async-start(bf16[8,64,256]{2,1,0:T(8,128)(2,1)} %bitcast.26), calls=%async_computation.2 | async-start | bytes 524288 | tf_op jit(solution)/shard_map/all_to_all | solution.py:110
  65.9 4.6 %all-to-all-done.2 = bf16[8,64,256]{2,1,0:T(8,128)(2,1)S(1)} async-done(((bf16[8,64,256]{2,1,0:T(8,128)(2,1)}), bf16[8,64,256]{2,1,0:T(8,128)(2,1)S(1)}, u32[]{:S(2)}, u32[]{:S(2)}) %all-to-all-start.2) | async-done | bytes 262176 | tf_op jit(solution)/shard_map/all_to_all | solution.py:110
  71.6 7.6 %collective-permute-done.1 = bf16[2,4,512,128]{3,2,1,0:T(8,128)(2,1)S(1)} collective-permute-done((bf16[2,4,512,128]{3,2,1,0:T(8,128)(2,1)}, bf16[2,4,512,128]{3,2,1,0:T(8,128)(2,1)S(1)}, u32[]{:S(2)}, u32[]{:S(2)}) %collective-permute-start.1) | collective-permute-done | bytes 1048608 | tf_op jit(solution)/shard_map/ppermute | solution.py:24
  81.7 20.3 %collective-permute-done = bf16[2,4,512,128]{3,2,1,0:T(8,128)(2,1)} collective-permute-done((bf16[2,4,512,128]{3,2,1,0:T(8,128)(2,1)}, bf16[2,4,512,128]{3,2,1,0:T(8,128)(2,1)}, u32[]{:S(2)}, u32[]{:S(2)}) %collective-permute-start) | collective-permute-done | bytes 1048608 | tf_op jit(solution)/shard_map/ppermute | solution.py:22
  102.0 2.7 reshape.427
  109.0 3.1 gather_fusion.7
  112.8 3.0 gather_fusion.8
  115.9 6.7 %fusion.11 = f32[8,4,1024,64]{2,3,1,0:T(8,128)} fusion(bf16[8,8,4,8,8,128]{5,4,3,2,1,0:T(8,128)(2,1)} %bitcast.216, bf16[1,8,64,4,64]{4,3,2,1,0:T(4,128)(2,1)S(1)} %copy-done.4), kind=kOutput, calls=%fused_computation.27 | convolution fusion | flops 268435456 | bytes 12845056 | tf_op jit(solution)/shard_map/while/body/eval_jaxpr/bhqe,hbke->bhqk/dot_general | solution.py:50
  122.5 8.4 %fusion.68 = (f32[8,4,64]{2,1,0:T(4,128)S(1)}, f32[8,4,64,1024]{3,2,1,0:T(8,128)S(1)}) fusion(f32[8,4,1024,64]{2,3,1,0:T(8,128)} %fusion.11, pred[8,1024]{1,0:T(8,128)(4,1)S(1)} %fusion.50), kind=kOutput, calls=%fused_computation.114 | output fusion | flops 12583935 | bytes 16793600 | tf_op jit(solution)/shard_map/while/body/eval_jaxpr/sub | solution.py:55
  135.3 4.5 %fusion.13 = f32[4,8,1024,64]{2,3,1,0:T(8,128)} fusion(bf16[8,4,64,1024]{3,2,1,0:T(8,128)(2,1)S(1)} %divide_convert_fusion, bf16[8,4,64,64]{2,3,1,0:T(8,128)(2,1)S(1)} %get-tuple-element.35), kind=kOutput, calls=%fused_computation.29 | convolution fusion | flops 268435456 | bytes 12845056 | tf_op jit(solution)/shard_map/while/body/eval_jaxpr/bhqk,bhqe->hbke/dot_general | solution.py:76
  144.9 8.1 %copy.197 = f32[4,8,1024,64]{2,1,3,0:T(8,128)} copy(f32[4,8,1024,64]{2,3,1,0:T(8,128)S(1)} %broadcast_multiply_fusion) | data formatting | bytes 16777216 | tf_op jit(solution)/shard_map/while/body/eval_jaxpr/mul | solution.py:74
  153.0 9.6 %reshape.524 = f32[4,64,128,64]{2,1,3,0:T(8,128)} reshape(f32[4,8,1024,64]{2,1,3,0:T(8,128)} %copy.197) | data formatting | bytes 16777216 | tf_op jit(solution)/shard_map/while/body/eval_jaxpr/reshape | solution.py:81
  162.6 11.5 %copy.198 = f32[64,4,128,64]{2,3,1,0:T(8,128)} copy(f32[64,4,128,64]{2,0,3,1:T(8,128)} %bitcast.220) | data formatting | bytes 16777216 | tf_op jit(solution)/shard_map/while/body/eval_jaxpr/reshape | solution.py:81
  174.5 13.4 %scatter_fusion = f32[4,24,128,64]{2,3,1,0:T(8,128)S(1)} fusion(f32[4,24,128,64]{2,3,1,0:T(8,128)S(1)} %broadcast.273.clone, s32[64]{0:T(128)S(1)} %reshape.485, f32[64,4,128,64]{2,3,1,0:T(8,128)} %copy.198), kind=kCustom, calls=%fused_computation.9 | custom fusion | flops 2097152 | bytes 25166080 | tf_op jit(solution)/shard_map/while/body/eval_jaxpr/scatter-add | solution.py:80
  187.8 3.5 copy.199
  191.4 3.0 stack.19
  196.2 11.5 %copy.202 = f32[4,8,1024,64]{2,1,3,0:T(8,128)} copy(f32[4,8,1024,64]{2,3,1,0:T(8,128)} %fusion.13) | data formatting | bytes 16777216 | tf_op jit(solution)/shard_map/while/body/eval_jaxpr/bhqk,bhqe->hbke/dot_general | solution.py:76
  207.7 9.3 %reshape.532 = f32[4,64,128,64]{2,1,3,0:T(8,128)} reshape(f32[4,8,1024,64]{2,1,3,0:T(8,128)} %copy.202) | data formatting | bytes 16777216 | tf_op jit(solution)/shard_map/while/body/eval_jaxpr/reshape | solution.py:84
  217.0 11.5 %copy.203 = f32[64,4,128,64]{2,3,1,0:T(8,128)} copy(f32[64,4,128,64]{2,0,3,1:T(8,128)} %bitcast.221) | data formatting | bytes 16777216 | tf_op jit(solution)/shard_map/while/body/eval_jaxpr/reshape | solution.py:84
  228.9 13.6 %scatter_fusion.1 = f32[4,24,128,64]{2,3,1,0:T(8,128)S(1)} fusion(f32[4,24,128,64]{2,3,1,0:T(8,128)S(1)} %broadcast.273.clone.1, s32[64]{0:T(128)S(1)} %reshape.485, f32[64,4,128,64]{2,3,1,0:T(8,128)} %copy.203), kind=kCustom, calls=%fused_computation.10 | custom fusion | flops 2097152 | bytes 25166080 | tf_op jit(solution)/shard_map/while/body/eval_jaxpr/scatter-add | solution.py:83
  242.4 3.5 copy.204
  245.9 2.8 stack.20
  250.6 4.6 %slice.77 = f32[2,4,2048,64]{2,3,1,0:T(8,128)} slice(f32[2,4,3072,64]{2,3,1,0:T(8,128)} %constant_dynamic-update-slice_fusion), slice={[0:2], [0:4], [1024:3072], [0:64]} | slice | bytes 8388608 | tf_op jit(solution)/shard_map/slice | solution.py:193
  255.3 6.9 %copy.205 = f32[2,4,2048,64]{3,2,1,0:T(8,128)} copy(f32[2,4,2048,64]{2,3,1,0:T(8,128)} %slice.77) | data formatting | bytes 8388608 | tf_op jit(solution)/shard_map/slice | solution.py:193
  262.2 7.2 %reshape.446 = f32[2,4,1024,128]{3,2,1,0:T(8,128)} reshape(f32[2,4,2048,64]{3,2,1,0:T(8,128)} %copy.205) | data formatting | bytes 8388608 | tf_op jit(solution)/shard_map/reshape | solution.py:193
  269.4 4.8 %fusion.64 = (f32[2,4,512,128]{3,2,1,0:T(8,128)}, f32[2,4,512,128]{3,2,1,0:T(8,128)}) fusion(f32[2,4,1024,128]{3,2,1,0:T(8,128)} %reshape.446), kind=kLoop, calls=%fused_computation.110 | loop fusion | bytes 8388608 | tf_op jit(solution)/shard_map/slice | solution.py:18
  279.0 4.1 all-to-all-start.3
  283.1 4.7 %fusion.40 = bf16[1,8,64,4,64]{4,2,3,1,0:T(8,128)(2,1)S(1)} fusion(bf16[8,4,64,1024]{3,2,1,0:T(8,128)(2,1)} %copy-done.3, bf16[8,8,4,8,8,128]{5,4,3,2,1,0:T(8,128)(2,1)} %bitcast.217), kind=kOutput, calls=%fused_computation.51 | convolution fusion | flops 268697600 | bytes 8650752 | tf_op jit(solution)/shard_map/while/body/eval_jaxpr/bhqk,hbke->bhqe/dot_general | solution.py:70
  291.1 33.7 %collective-permute-done.2 = f32[2,4,512,128]{3,2,1,0:T(8,128)} collective-permute-done((f32[2,4,512,128]{3,2,1,0:T(8,128)}, f32[2,4,512,128]{3,2,1,0:T(8,128)}, u32[]{:S(2)}, u32[]{:S(2)}) %collective-permute-start.2) | collective-permute-done | bytes 2097184 | tf_op jit(solution)/shard_map/ppermute | solution.py:22
  324.8 4.4 %reshape.540 = f32[2,4,8,128,64]{4,3,2,1,0:T(8,128)} reshape(f32[2,4,512,128]{3,2,1,0:T(8,128)} %collective-permute-done.2) | data formatting | bytes 4194304 | tf_op jit(solution)/shard_map/reshape | solution.py:195
  329.2 3.8 copy.207
  333.0 34.6 %collective-permute-done.3 = f32[2,4,512,128]{3,2,1,0:T(8,128)} collective-permute-done((f32[2,4,512,128]{3,2,1,0:T(8,128)}, f32[2,4,512,128]{3,2,1,0:T(8,128)}, u32[]{:S(2)}, u32[]{:S(2)}) %collective-permute-start.3) | collective-permute-done | bytes 2097184 | tf_op jit(solution)/shard_map/ppermute | solution.py:24
  367.6 4.4 %reshape.548 = f32[2,4,8,128,64]{4,3,2,1,0:T(8,128)} reshape(f32[2,4,512,128]{3,2,1,0:T(8,128)} %collective-permute-done.3) | data formatting | bytes 4194304 | tf_op jit(solution)/shard_map/reshape | solution.py:196
  372.0 3.8 copy.208
  375.8 3.5 scatter_fusion.2
  379.3 3.5 scatter_fusion.3
  382.8 3.6 all-to-all-start.5
  388.9 4.4 %all-to-all-done.5 = bf16[8,64,256]{2,1,0:T(8,128)(2,1)S(1)} async-done(((bf16[8,64,256]{2,1,0:T(8,128)(2,1)}), bf16[8,64,256]{2,1,0:T(8,128)(2,1)S(1)}, u32[]{:S(2)}, u32[]{:S(2)}) %all-to-all-start.5) | async-done | bytes 262176 | tf_op jit(solution)/shard_map/all_to_all | solution.py:217
  393.3 3.6 all-to-all-start.6
  398.8 24.6 %all-to-all-done.6 = f32[2,8,128,256]{2,3,0,1:T(8,128)S(1)} async-done(((f32[2,8,128,256]{2,3,0,1:T(8,128)}), f32[2,8,128,256]{2,3,0,1:T(8,128)S(1)}, u32[]{:S(2)}, u32[]{:S(2)}) %all-to-all-start.6) | async-done | bytes 2097184 | tf_op jit(solution)/shard_map/all_to_all | solution.py:204
  (113 shorter events, 58.9 us)
Async XLA Ops:
  0.6 23.2 %copy-start = (s32[1,8,8]{2,1,0:T(8,128)S(1)}, s32[1,8,8]{2,1,0:T(8,128)}, u32[]{:S(2)}) copy-start(s32[1,8,8]{2,1,0:T(8,128)} %param.11) | copy-start | bytes 772
  0.6 22.3 %copy-start.8 = (bf16[128,1024]{1,0:T(8,128)(2,1)S(1)}, bf16[128,1024]{1,0:T(8,128)(2,1)}, u32[]{:S(2)}) copy-start(bf16[128,1024]{1,0:T(8,128)(2,1)} %param.10) | copy-start | bytes 786436
  3.0 14.9 %all-to-all-start.1 = ((bf16[8,128,256]{1,2,0:T(8,128)(2,1)}), bf16[8,128,256]{1,2,0:T(8,128)(2,1)S(1)}, u32[]{:S(2)}, u32[]{:S(2)}) async-start(bf16[8,128,256]{1,2,0:T(8,128)(2,1)} %bitcast.15), calls=%async_computation.1 | async-start | bytes 1048576 | tf_op jit(solution)/shard_map/all_to_all | solution.py:120
  11.1 13.4 %copy-start.9 = (s32[8]{0:T(128)}, s32[8]{0:T(128)S(1)}, u32[]{:S(2)}) copy-start(s32[8]{0:T(128)S(1)} %get-tuple-element.65) | copy-start | bytes 100
  11.1 13.4 %copy-start.11 = (s32[8]{0:T(128)}, s32[8]{0:T(128)S(1)}, u32[]{:S(2)}) copy-start(s32[8]{0:T(128)S(1)} %get-tuple-element.64) | copy-start | bytes 100
  18.7 13.1 %all-to-all-start = ((bf16[8,128,256]{1,2,0:T(8,128)(2,1)}), bf16[8,128,256]{1,2,0:T(8,128)(2,1)S(1)}, u32[]{:S(2)}, u32[]{:S(2)}) async-start(bf16[8,128,256]{1,2,0:T(8,128)(2,1)} %bitcast.13), calls=%async_computation | async-start | bytes 1048576 | tf_op jit(solution)/shard_map/all_to_all | solution.py:119
  31.9 27.4 %all-to-all-start.4 = ((bf16[8,64,256]{2,1,0:T(8,128)(2,1)}), bf16[8,64,256]{2,1,0:T(8,128)(2,1)S(1)}, u32[]{:S(2)}, u32[]{:S(2)}) async-start(bf16[8,64,256]{2,1,0:T(8,128)(2,1)} %bitcast.38), calls=%async_computation.4 | async-start | bytes 524288 | tf_op jit(solution)/shard_map/all_to_all | solution.py:111
  51.7 27.5 %collective-permute-start.1 = (bf16[2,4,512,128]{3,2,1,0:T(8,128)(2,1)}, bf16[2,4,512,128]{3,2,1,0:T(8,128)(2,1)S(1)}, u32[]{:S(2)}, u32[]{:S(2)}) collective-permute-start(bf16[2,4,512,128]{3,2,1,0:T(8,128)(2,1)} %get-tuple-element.54), channel_id=1, source_target_pairs={{8,0},{16,8},{24,16},{0,24},{9,1},{17,9},{25,17},{1,25},{10,2},{18... | collective-permute-start | bytes 3145736 | tf_op jit(solution)/shard_map/ppermute | solution.py:24
  55.3 46.7 %collective-permute-start = (bf16[2,4,512,128]{3,2,1,0:T(8,128)(2,1)}, bf16[2,4,512,128]{3,2,1,0:T(8,128)(2,1)}, u32[]{:S(2)}, u32[]{:S(2)}) collective-permute-start(bf16[2,4,512,128]{3,2,1,0:T(8,128)(2,1)} %get-tuple-element.53), channel_id=1, source_target_pairs={{0,8},{8,16},{16,24},{24,0},{1,9},{9,17},{17,25},{25,1},{2,10},{10... | collective-permute-start | bytes 3145736 | tf_op jit(solution)/shard_map/ppermute | solution.py:22
  59.3 11.2 %all-to-all-start.2 = ((bf16[8,64,256]{2,1,0:T(8,128)(2,1)}), bf16[8,64,256]{2,1,0:T(8,128)(2,1)S(1)}, u32[]{:S(2)}, u32[]{:S(2)}) async-start(bf16[8,64,256]{2,1,0:T(8,128)(2,1)} %bitcast.26), calls=%async_computation.2 | async-start | bytes 524288 | tf_op jit(solution)/shard_map/all_to_all | solution.py:110
  80.1 26.3 %copy-start.5 = (bf16[2,4,1024,64]{2,3,1,0:T(8,128)(2,1)S(1)}, bf16[2,4,1024,64]{2,3,1,0:T(8,128)(2,1)}, u32[]{:S(2)}) copy-start(bf16[2,4,1024,64]{2,3,1,0:T(8,128)(2,1)} %get-tuple-element.55) | copy-start | bytes 3145732
  112.8 3.1 copy-start.4
  131.0 2.2 copy-start.2
  131.0 2.3 copy-start.7
  141.6 1.9 copy-start.3
  269.4 8.6 %copy-start.6 = (bf16[8,4,64,64]{2,3,1,0:T(8,128)(2,1)S(1)}, bf16[8,4,64,64]{2,3,1,0:T(8,128)(2,1)}, u32[]{:S(2)}) copy-start(bf16[8,4,64,64]{2,3,1,0:T(8,128)(2,1)} %get-tuple-element.68) | copy-start | bytes 786436
  274.2 50.6 %collective-permute-start.2 = (f32[2,4,512,128]{3,2,1,0:T(8,128)}, f32[2,4,512,128]{3,2,1,0:T(8,128)}, u32[]{:S(2)}, u32[]{:S(2)}) collective-permute-start(f32[2,4,512,128]{3,2,1,0:T(8,128)} %get-tuple-element.37), channel_id=1, source_target_pairs={{0,8},{8,16},{16,24},{24,0},{1,9},{9,17},{17,25},{25,1},{2,10},{10... | collective-permute-start | bytes 6291464 | tf_op jit(solution)/shard_map/ppermute | solution.py:22
  275.6 92.1 %collective-permute-start.3 = (f32[2,4,512,128]{3,2,1,0:T(8,128)}, f32[2,4,512,128]{3,2,1,0:T(8,128)}, u32[]{:S(2)}, u32[]{:S(2)}) collective-permute-start(f32[2,4,512,128]{3,2,1,0:T(8,128)} %get-tuple-element.36), channel_id=1, source_target_pairs={{8,0},{16,8},{24,16},{0,24},{9,1},{17,9},{25,17},{1,25},{10,2},{18... | collective-permute-start | bytes 6291464 | tf_op jit(solution)/shard_map/ppermute | solution.py:24
  279.0 103.9 %all-to-all-start.3 = ((bf16[8,64,256]{2,1,0:T(8,128)(2,1)}), bf16[8,64,256]{2,1,0:T(8,128)(2,1)S(1)}, u32[]{:S(2)}, u32[]{:S(2)}) async-start(bf16[8,64,256]{2,1,0:T(8,128)(2,1)} %copy.186), calls=%async_computation.3 | async-start | bytes 524288 | tf_op jit(solution)/shard_map/all_to_all | solution.py:216
  372.0 3.8 copy-start.12
  375.8 3.5 copy-start.10
  382.8 10.5 %all-to-all-start.5 = ((bf16[8,64,256]{2,1,0:T(8,128)(2,1)}), bf16[8,64,256]{2,1,0:T(8,128)(2,1)S(1)}, u32[]{:S(2)}, u32[]{:S(2)}) async-start(bf16[8,64,256]{2,1,0:T(8,128)(2,1)} %reshape.440), calls=%async_computation.5 | async-start | bytes 524288 | tf_op jit(solution)/shard_map/all_to_all | solution.py:217
  393.3 30.2 %all-to-all-start.6 = ((f32[2,8,128,256]{2,3,0,1:T(8,128)}), f32[2,8,128,256]{2,3,0,1:T(8,128)S(1)}, u32[]{:S(2)}, u32[]{:S(2)}) async-start(f32[2,8,128,256]{2,3,0,1:T(8,128)} %copy.210), calls=%async_computation.6 | async-start | bytes 4194304 | tf_op jit(solution)/shard_map/all_to_all | solution.py:204
  397.1 28.8 %copy-start.1 = (s32[1,8,8]{2,1,0:T(8,128)S(1)}, s32[1,8,8]{2,1,0:T(8,128)}, u32[]{:S(2)}) copy-start(s32[1,8,8]{2,1,0:T(8,128)} %param.11) | copy-start | bytes 772
where the time goes:
time: 434 us; the launch traced here: 426 us
  local copies, waits for them, and re-layouts  176 us (41%)
  waiting for transfers between devices  144 us (33%)
  other arithmetic  48.8 us (11%)
  starting transfers between devices  35.2 us (8%)
  matrix products  21 us (5%)
    ppermute x2, waiting for transfers between devices, with_halo(): lax.ppermute(tail, axis, [(i, (i + 1) % count) for i in range(count)])  54 us
    ppermute x2, waiting for transfers between devices, with_halo(): lax.ppermute(head, axis, [((i + 1) % count, i) for i in range(count)])  42.2 us
    all_to_all x1, waiting for transfers between devices, body(): lax.all_to_all(inner.reshape(2, seq_count, galaxies, pair_width), 'seq',...  24.6 us
    reshape x2, local copies, waits for them, and re-layouts, attend_group(): key_part.reshape(heads, group_size * neighbours, block_len, depth)  21.1 us
    reshape x2, local copies, waits for them, and re-layouts, attend_group(): value_part.reshape(heads, group_size * neighbours, block_len, depth)  20.8 us
    scatter-add x1, other arithmetic, attend_group(): value_acc.at[:, flat_ids]  13.6 us
    scatter-add x1, other arithmetic, attend_group(): key_acc.at[:, flat_ids]  13.4 us
    slice x2, local copies, waits for them, and re-layouts, body(): rim_out = accum[:, :, region_rows:].reshape(2, pair_heads, rim_rows, 2 * HD)  11.6 us
  transfers between devices with their start and end apart: 11, of which 9 were waited for; matrix products, arithmetic and copies ran while one was open for 16% of the time, Pallas kernels for 0%

commit v1 on v0

--- a/solution.py
+++ b/solution.py
@@ -4,12 +4,31 @@
 import jax.numpy as jnp
 from jax import lax
 from jax.sharding import PartitionSpec as P
+from jax.lax import axis_index, axis_size, ppermute
 
 H = 16
 HD = 64
 BLK = 128
 NBR = 8
 BND = 8
+
+
+def area_manage(w_in, join_dim, local_array):
+    res = w_in.shape
+    v1 = w_in.reshape(
+        *res[:join_dim], local_array, res[join_dim] // local_array, *res[join_dim + 1 :]
+    )
+    m_next = jnp.moveaxis(v1, join_dim, 0)
+    return m_next
+
+
+def push_seats_all(frame, out_dim):
+    frame = jnp.moveaxis(frame, 0, out_dim)
+    b_now = frame.shape
+    x_now = frame.reshape(
+        *b_now[:out_dim], b_now[out_dim] * b_now[out_dim + 1], *b_now[out_dim + 2 :]
+    )
+    return x_now
 
 
 def with_halo(cells, sides, width):
@@ -115,9 +134,24 @@
         grouped = matrix.reshape(galaxies, pair_count, pair_width).transpose(1, 0, 2)
         return jnp.repeat(grouped, 2, axis=0)
 
+    def end_the_task(sample, ax_name, local_x, s0):
+        heard = axis_size(ax_name)
+        clean, outcome_arr = (heard, axis_index(ax_name))
+        mat_out = area_manage(sample, local_x, clean)
+        rows = [mat_out[outcome_arr]]
+        q = 1
+        while q < clean:
+            out_arr = mat_out[(outcome_arr + q) % clean]
+            rows.append(ppermute(out_arr, ax_name, [(k0, (k0 + q) % clean) for k0 in range(clean)]))
+            q += 1
+        o_now = jnp.stack(rows, axis=0)
+        mat_out = o_now[(outcome_arr - jnp.arange(clean)) % clean]
+        local_out = push_seats_all(mat_out, s0)
+        return local_out
+
     key_heads, value_heads = (
         lax.all_to_all(all_slots(keys), "seq", split_axis=0, concat_axis=1, tiled=True),
-        lax.all_to_all(all_slots(values), "seq", split_axis=0, concat_axis=1, tiled=True),
+        end_the_task(all_slots(values), "seq", 0, 1),
     )
     paired = jnp.stack([key_heads[0], value_heads[0]])
     head_first = paired.reshape(2, region_rows, pair_heads, HD).transpose(0, 2, 1, 3)

time: 434 us -> 428 us (0.986)
  waiting for transfers between devices: 144 us -> 135 us
  starting transfers between devices: 35.2 us -> 39.8 us
    ppermute x0 -> x7, starting transfers between devices: none -> 9.54 us  [end_the_task(): ppermute(out_arr, ax_name, [(k0, (k0 + q) % clean) for k0 in range(clean)])]
    all_to_all x1, waiting for transfers between devices: 6.82 us -> 0.01 us  [body(): lax.all_to_all(all_slots(keys), 'seq', split_axis=0, concat_axis=1, tiled...]
    all_to_all x1 -> x0, waiting for transfers between devices: 6.78 us -> none  [body(): lax.all_to_all(all_slots(values), 'seq', split_axis=0, concat_axis=1, til...]
    all_to_all x1 -> x0, starting transfers between devices: 5.2 us -> none  [body(): lax.all_to_all(all_slots(values), 'seq', split_axis=0, concat_axis=1, til...]
    ppermute x0 -> x7, waiting for transfers between devices: none -> 4.88 us  [end_the_task(): ppermute(out_arr, ax_name, [(k0, (k0 + q) % clean) for k0 in range(clean)])]
    unnamed x35 -> x45, local copies, waits for them, and re-layouts: 9.73 us -> 9.78 us
  transfers between devices with their start and end apart: 11 -> 17, of which waited for: 9 -> 8; matrix products, arithmetic and copies ran while one was open for 16% -> 16% of each run, Pallas kernels for 0% -> 0%
where the time goes in v1:
time: 428 us; the launch traced here: 420 us
  local copies, waits for them, and re-layouts  174 us (41%)
  waiting for transfers between devices  135 us (32%)
  other arithmetic  48.1 us (11%)
  starting transfers between devices  39.8 us (9%)
  matrix products  21.1 us (5%)
    ppermute x2, waiting for transfers between devices, with_halo(): lax.ppermute(tail, axis, [(i, (i + 1) % count) for i in range(count)])  54.1 us
    ppermute x2, waiting for transfers between devices, with_halo(): lax.ppermute(head, axis, [((i + 1) % count, i) for i in range(count)])  42.3 us
    all_to_all x1, waiting for transfers between devices, body(): lax.all_to_all(inner.reshape(2, seq_count, galaxies, pair_width), 'seq',...  24.6 us
    reshape x2, local copies, waits for them, and re-layouts, attend_group(): key_part.reshape(heads, group_size * neighbours, block_len, depth)  21.1 us
    reshape x2, local copies, waits for them, and re-layouts, attend_group(): value_part.reshape(heads, group_size * neighbours, block_len, depth)  20.8 us
    scatter-add x1, other arithmetic, attend_group(): value_acc.at[:, flat_ids]  13.6 us
    scatter-add x1, other arithmetic, attend_group(): key_acc.at[:, flat_ids]  13.4 us
    slice x2, local copies, waits for them, and re-layouts, body(): rim_out = accum[:, :, region_rows:].reshape(2, pair_heads, rim_rows, 2 * HD)  11.6 us
  transfers between devices with their start and end apart: 17, of which 8 were waited for; matrix products, arithmetic and copies ran while one was open for 16% of the time, Pallas kernels for 0%

profile of v1, /device:TPU:0, one launch (start us, length us, event | category | flops | bytes accessed | tf_op | source)
XLA Modules:
  0.0 420.2 jit_solution(555018767856405622)
XLA Ops:
  2.6 2.5 collective-permute-start.1
  10.4 3.9 all-to-all-start
  16.1 3.0 collective-permute-start.5
  19.6 4.9 %collective-permute-done.5 = bf16[1,128,256]{2,1,0:T(8,128)(2,1)S(1)} collective-permute-done((bf16[1,128,256]{2,1,0:T(8,128)(2,1)S(1)}, bf16[1,128,256]{2,1,0:T(8,128)(2,1)S(1)}, u32[]{:S(2)}, u32[]{:S(2)}) %collective-permute-start.5) | collective-permute-done | bytes 65568 | tf_op jit(solution)/shard_map/ppermute | solution.py:145
  25.7 3.4 all-to-all-start.3
  34.1 4.8 %copy.177 = bf16[2,4,16,128,64]{4,3,2,1,0:T(8,128)(2,1)} copy(bf16[2,4,16,128,64]{3,4,1,0,2:T(8,128)(2,1)} %pad_maximum_fusion.1) | data formatting | bytes 4194304 | tf_op jit(solution)/shard_map/concatenate | solution.py:164
  38.9 5.0 %reshape.468 = bf16[2,4,1024,128]{3,2,1,0:T(8,128)(2,1)S(1)} reshape(bf16[2,4,16,128,64]{4,3,2,1,0:T(8,128)(2,1)} %copy.177) | data formatting | bytes 4194304 | tf_op jit(solution)/shard_map/reshape | solution.py:166
  45.5 3.6 collective-permute-start.8
  53.0 4.3 %all-to-all-start.1 = ((bf16[8,64,256]{2,1,0:T(8,128)(2,1)}), bf16[8,64,256]{2,1,0:T(8,128)(2,1)S(1)}, u32[]{:S(2)}, u32[]{:S(2)}) async-start(bf16[8,64,256]{2,1,0:T(8,128)(2,1)} %bitcast.42), calls=%async_computation.1 | async-start | bytes 524288 | tf_op jit(solution)/shard_map/all_to_all | solution.py:129
  59.6 4.6 %all-to-all-done.1 = bf16[8,64,256]{2,1,0:T(8,128)(2,1)S(1)} async-done(((bf16[8,64,256]{2,1,0:T(8,128)(2,1)}), bf16[8,64,256]{2,1,0:T(8,128)(2,1)S(1)}, u32[]{:S(2)}, u32[]{:S(2)}) %all-to-all-start.1) | async-done | bytes 262176 | tf_op jit(solution)/shard_map/all_to_all | solution.py:129
  65.3 7.7 %collective-permute-done.8 = bf16[2,4,512,128]{3,2,1,0:T(8,128)(2,1)S(1)} collective-permute-done((bf16[2,4,512,128]{3,2,1,0:T(8,128)(2,1)}, bf16[2,4,512,128]{3,2,1,0:T(8,128)(2,1)S(1)}, u32[]{:S(2)}, u32[]{:S(2)}) %collective-permute-start.8) | collective-permute-done | bytes 1048608 | tf_op jit(solution)/shard_map/ppermute | solution.py:43
  75.4 20.4 %collective-permute-done.7 = bf16[2,4,512,128]{3,2,1,0:T(8,128)(2,1)} collective-permute-done((bf16[2,4,512,128]{3,2,1,0:T(8,128)(2,1)}, bf16[2,4,512,128]{3,2,1,0:T(8,128)(2,1)}, u32[]{:S(2)}, u32[]{:S(2)}) %collective-permute-start.7) | collective-permute-done | bytes 1048608 | tf_op jit(solution)/shard_map/ppermute | solution.py:41
  95.8 2.7 reshape.469
  102.8 3.1 gather_fusion.8
  106.7 3.1 gather_fusion.9
  109.7 6.7 %fusion.11 = f32[8,4,1024,64]{2,3,1,0:T(8,128)} fusion(bf16[8,8,4,8,8,128]{5,4,3,2,1,0:T(8,128)(2,1)} %bitcast.243, bf16[1,8,64,4,64]{4,3,2,1,0:T(4,128)(2,1)S(1)} %copy-done.4), kind=kOutput, calls=%fused_computation.28 | convolution fusion | flops 268435456 | bytes 12845056 | tf_op jit(solution)/shard_map/while/body/eval_jaxpr/bhqe,hbke->bhqk/dot_general | solution.py:69
  116.4 8.4 %fusion.70 = (f32[8,4,64]{2,1,0:T(4,128)S(1)}, f32[8,4,64,1024]{3,2,1,0:T(8,128)S(1)}) fusion(f32[8,4,1024,64]{2,3,1,0:T(8,128)} %fusion.11, pred[8,1024]{1,0:T(8,128)(4,1)S(1)} %fusion.50), kind=kOutput, calls=%fused_computation.137 | output fusion | flops 12583935 | bytes 16793600 | tf_op jit(solution)/shard_map/while/body/eval_jaxpr/sub | solution.py:74
  129.2 4.5 %fusion.13 = f32[4,8,1024,64]{2,3,1,0:T(8,128)} fusion(bf16[8,4,64,1024]{3,2,1,0:T(8,128)(2,1)S(1)} %divide_convert_fusion, bf16[8,4,64,64]{2,3,1,0:T(8,128)(2,1)S(1)} %get-tuple-element.35), kind=kOutput, calls=%fused_computation.30 | convolution fusion | flops 268435456 | bytes 12845056 | tf_op jit(solution)/shard_map/while/body/eval_jaxpr/bhqk,bhqe->hbke/dot_general | solution.py:95
  138.8 8.1 %copy.199 = f32[4,8,1024,64]{2,1,3,0:T(8,128)} copy(f32[4,8,1024,64]{2,3,1,0:T(8,128)S(1)} %broadcast_multiply_fusion) | data formatting | bytes 16777216 | tf_op jit(solution)/shard_map/while/body/eval_jaxpr/mul | solution.py:93
  147.0 9.6 %reshape.576 = f32[4,64,128,64]{2,1,3,0:T(8,128)} reshape(f32[4,8,1024,64]{2,1,3,0:T(8,128)} %copy.199) | data formatting | bytes 16777216 | tf_op jit(solution)/shard_map/while/body/eval_jaxpr/reshape | solution.py:100
  156.6 11.5 %copy.200 = f32[64,4,128,64]{2,3,1,0:T(8,128)} copy(f32[64,4,128,64]{2,0,3,1:T(8,128)} %bitcast.247) | data formatting | bytes 16777216 | tf_op jit(solution)/shard_map/while/body/eval_jaxpr/reshape | solution.py:100
  168.5 13.4 %scatter_fusion = f32[4,24,128,64]{2,3,1,0:T(8,128)S(1)} fusion(f32[4,24,128,64]{2,3,1,0:T(8,128)S(1)} %broadcast.338.clone, s32[64]{0:T(128)S(1)} %reshape.527, f32[64,4,128,64]{2,3,1,0:T(8,128)} %copy.200), kind=kCustom, calls=%fused_computation.10 | custom fusion | flops 2097152 | bytes 25166080 | tf_op jit(solution)/shard_map/while/body/eval_jaxpr/scatter-add | solution.py:99
  181.8 3.5 copy.201
  185.4 3.0 stack.51
  190.2 11.5 %copy.204 = f32[4,8,1024,64]{2,1,3,0:T(8,128)} copy(f32[4,8,1024,64]{2,3,1,0:T(8,128)} %fusion.13) | data formatting | bytes 16777216 | tf_op jit(solution)/shard_map/while/body/eval_jaxpr/bhqk,bhqe->hbke/dot_general | solution.py:95
  201.7 9.3 %reshape.584 = f32[4,64,128,64]{2,1,3,0:T(8,128)} reshape(f32[4,8,1024,64]{2,1,3,0:T(8,128)} %copy.204) | data formatting | bytes 16777216 | tf_op jit(solution)/shard_map/while/body/eval_jaxpr/reshape | solution.py:103
  211.0 11.5 %copy.205 = f32[64,4,128,64]{2,3,1,0:T(8,128)} copy(f32[64,4,128,64]{2,0,3,1:T(8,128)} %bitcast.248) | data formatting | bytes 16777216 | tf_op jit(solution)/shard_map/while/body/eval_jaxpr/reshape | solution.py:103
  222.8 13.6 %scatter_fusion.1 = f32[4,24,128,64]{2,3,1,0:T(8,128)S(1)} fusion(f32[4,24,128,64]{2,3,1,0:T(8,128)S(1)} %broadcast.338.clone.1, s32[64]{0:T(128)S(1)} %reshape.527, f32[64,4,128,64]{2,3,1,0:T(8,128)} %copy.205), kind=kCustom, calls=%fused_computation.11 | custom fusion | flops 2097152 | bytes 25166080 | tf_op jit(solution)/shard_map/while/body/eval_jaxpr/scatter-add | solution.py:102
  236.4 3.4 copy.206
  239.9 2.8 stack.52
  244.6 4.7 %slice.79 = f32[2,4,2048,64]{2,3,1,0:T(8,128)} slice(f32[2,4,3072,64]{2,3,1,0:T(8,128)} %constant_dynamic-update-slice_fusion), slice={[0:2], [0:4], [1024:3072], [0:64]} | slice | bytes 8388608 | tf_op jit(solution)/shard_map/slice | solution.py:227
  249.2 7.0 %copy.207 = f32[2,4,2048,64]{3,2,1,0:T(8,128)} copy(f32[2,4,2048,64]{2,3,1,0:T(8,128)} %slice.79) | data formatting | bytes 8388608 | tf_op jit(solution)/shard_map/slice | solution.py:227
  256.2 7.2 %reshape.488 = f32[2,4,1024,128]{3,2,1,0:T(8,128)} reshape(f32[2,4,2048,64]{3,2,1,0:T(8,128)} %copy.207) | data formatting | bytes 8388608 | tf_op jit(solution)/shard_map/reshape | solution.py:227
  263.4 4.8 %fusion.66 = (f32[2,4,512,128]{3,2,1,0:T(8,128)}, f32[2,4,512,128]{3,2,1,0:T(8,128)}) fusion(f32[2,4,1024,128]{3,2,1,0:T(8,128)} %reshape.488), kind=kLoop, calls=%fused_computation.133 | loop fusion | bytes 8388608 | tf_op jit(solution)/shard_map/slice | solution.py:37
  273.0 4.1 all-to-all-start.2
  277.1 4.7 %fusion.40 = bf16[1,8,64,4,64]{4,2,3,1,0:T(8,128)(2,1)S(1)} fusion(bf16[8,4,64,1024]{3,2,1,0:T(8,128)(2,1)} %copy-done.3, bf16[8,8,4,8,8,128]{5,4,3,2,1,0:T(8,128)(2,1)} %bitcast.244), kind=kOutput, calls=%fused_computation.52 | convolution fusion | flops 268697600 | bytes 8650752 | tf_op jit(solution)/shard_map/while/body/eval_jaxpr/bhqk,hbke->bhqe/dot_general | solution.py:89
  285.1 33.7 %collective-permute-done.9 = f32[2,4,512,128]{3,2,1,0:T(8,128)} collective-permute-done((f32[2,4,512,128]{3,2,1,0:T(8,128)}, f32[2,4,512,128]{3,2,1,0:T(8,128)}, u32[]{:S(2)}, u32[]{:S(2)}) %collective-permute-start.9) | collective-permute-done | bytes 2097184 | tf_op jit(solution)/shard_map/ppermute | solution.py:41
  318.9 4.3 %reshape.592 = f32[2,4,8,128,64]{4,3,2,1,0:T(8,128)} reshape(f32[2,4,512,128]{3,2,1,0:T(8,128)} %collective-permute-done.9) | data formatting | bytes 4194304 | tf_op jit(solution)/shard_map/reshape | solution.py:229
  323.2 3.9 copy.209
  327.1 34.6 %collective-permute-done.10 = f32[2,4,512,128]{3,2,1,0:T(8,128)} collective-permute-done((f32[2,4,512,128]{3,2,1,0:T(8,128)}, f32[2,4,512,128]{3,2,1,0:T(8,128)}, u32[]{:S(2)}, u32[]{:S(2)}) %collective-permute-start.10) | collective-permute-done | bytes 2097184 | tf_op jit(solution)/shard_map/ppermute | solution.py:43
  361.7 4.3 %reshape.600 = f32[2,4,8,128,64]{4,3,2,1,0:T(8,128)} reshape(f32[2,4,512,128]{3,2,1,0:T(8,128)} %collective-permute-done.10) | data formatting | bytes 4194304 | tf_op jit(solution)/shard_map/reshape | solution.py:230
  366.0 3.8 copy.210
  369.9 3.5 scatter_fusion.2
  373.3 3.5 scatter_fusion.3
  376.8 3.5 all-to-all-start.4
  382.8 4.4 %all-to-all-done.4 = bf16[8,64,256]{2,1,0:T(8,128)(2,1)S(1)} async-done(((bf16[8,64,256]{2,1,0:T(8,128)(2,1)}), bf16[8,64,256]{2,1,0:T(8,128)(2,1)S(1)}, u32[]{:S(2)}, u32[]{:S(2)}) %all-to-all-start.4) | async-done | bytes 262176 | tf_op jit(solution)/shard_map/all_to_all | solution.py:251
  387.2 3.6 all-to-all-start.5
  392.8 24.6 %all-to-all-done.5 = f32[2,8,128,256]{2,3,0,1:T(8,128)S(1)} async-done(((f32[2,8,128,256]{2,3,0,1:T(8,128)}), f32[2,8,128,256]{2,3,0,1:T(8,128)S(1)}, u32[]{:S(2)}, u32[]{:S(2)}) %all-to-all-start.5) | async-done | bytes 2097184 | tf_op jit(solution)/shard_map/all_to_all | solution.py:238
  (140 shorter events, 60.3 us)
Async XLA Ops:
  0.6 14.7 %copy-start = (s32[1,8,8]{2,1,0:T(8,128)S(1)}, s32[1,8,8]{2,1,0:T(8,128)}, u32[]{:S(2)}) copy-start(s32[1,8,8]{2,1,0:T(8,128)} %param.11) | copy-start | bytes 772
  0.6 13.7 %copy-start.8 = (bf16[128,1024]{1,0:T(8,128)(2,1)S(1)}, bf16[128,1024]{1,0:T(8,128)(2,1)}, u32[]{:S(2)}) copy-start(bf16[128,1024]{1,0:T(8,128)(2,1)} %param.10) | copy-start | bytes 786436
  0.7 14.6 %copy-start.14 = (s32[4,2,8]{2,1,0:T(2,128)S(1)}, s32[4,2,8]{2,1,0:T(2,128)}, u32[]{:S(2)}) copy-start(s32[4,2,8]{2,1,0:T(2,128)} %param.13) | copy-start | bytes 772
  0.7 15.4 %copy-start.13 = (s32[4,8]{1,0:T(4,128)S(1)}, s32[4,8]{1,0:T(4,128)}, u32[]{:S(2)}) copy-start(s32[4,8]{1,0:T(4,128)} %param.12) | copy-start | bytes 388
  2.1 14.0 %collective-permute-start = (bf16[1,128,256]{2,1,0:T(8,128)(2,1)S(1)}, bf16[1,128,256]{2,1,0:T(8,128)(2,1)S(1)}, u32[]{:S(2)}, u32[]{:S(2)}) collective-permute-start(bf16[1,128,256]{2,1,0:T(8,128)(2,1)S(1)} %get-tuple-element.65), channel_id=1, source_target_pairs={{0,1},{1,2},{2,3},{3,4},{4,5},{5,6},{6,7},{7,0},{8,9},{9,10},{10,1... | collective-permute-start | bytes 196616 | tf_op jit(solution)/shard_map/ppermute | solution.py:145
  2.6 16.4 %collective-permute-start.1 = (bf16[1,128,256]{2,1,0:T(8,128)(2,1)S(1)}, bf16[1,128,256]{2,1,0:T(8,128)(2,1)S(1)}, u32[]{:S(2)}, u32[]{:S(2)}) collective-permute-start(bf16[1,128,256]{2,1,0:T(8,128)(2,1)S(1)} %get-tuple-element.64), channel_id=1, source_target_pairs={{0,2},{1,3},{2,4},{3,5},{4,6},{5,7},{6,0},{7,1},{8,10},{9,11},{10,... | collective-permute-start | bytes 196616 | tf_op jit(solution)/shard_map/ppermute | solution.py:145
  5.2 14.4 %collective-permute-start.2 = (bf16[1,128,256]{2,1,0:T(8,128)(2,1)S(1)}, bf16[1,128,256]{2,1,0:T(8,128)(2,1)S(1)}, u32[]{:S(2)}, u32[]{:S(2)}) collective-permute-start(bf16[1,128,256]{2,1,0:T(8,128)(2,1)S(1)} %get-tuple-element.63), channel_id=1, source_target_pairs={{0,3},{1,4},{2,5},{3,6},{4,7},{5,0},{6,1},{7,2},{8,11},{9,12},{10,... | collective-permute-start | bytes 196616 | tf_op jit(solution)/shard_map/ppermute | solution.py:145
  7.5 12.0 %collective-permute-start.3 = (bf16[1,128,256]{2,1,0:T(8,128)(2,1)S(1)}, bf16[1,128,256]{2,1,0:T(8,128)(2,1)S(1)}, u32[]{:S(2)}, u32[]{:S(2)}) collective-permute-start(bf16[1,128,256]{2,1,0:T(8,128)(2,1)S(1)} %get-tuple-element.62), channel_id=1, source_target_pairs={{0,4},{1,5},{2,6},{3,7},{4,0},{5,1},{6,2},{7,3},{8,12},{9,13},{10,... | collective-permute-start | bytes 196616 | tf_op jit(solution)/shard_map/ppermute | solution.py:145
  8.1 11.6 %collective-permute-start.4 = (bf16[1,128,256]{2,1,0:T(8,128)(2,1)S(1)}, bf16[1,128,256]{2,1,0:T(8,128)(2,1)S(1)}, u32[]{:S(2)}, u32[]{:S(2)}) collective-permute-start(bf16[1,128,256]{2,1,0:T(8,128)(2,1)S(1)} %get-tuple-element.61), channel_id=1, source_target_pairs={{0,5},{1,6},{2,7},{3,0},{4,1},{5,2},{6,3},{7,4},{8,13},{9,14},{10,... | collective-permute-start | bytes 196616 | tf_op jit(solution)/shard_map/ppermute | solution.py:145
  10.4 15.2 %all-to-all-start = ((bf16[8,128,256]{1,2,0:T(8,128)(2,1)}), bf16[8,128,256]{1,2,0:T(8,128)(2,1)S(1)}, u32[]{:S(2)}, u32[]{:S(2)}) async-start(bf16[8,128,256]{1,2,0:T(8,128)(2,1)} %bitcast.13), calls=%async_computation | async-start | bytes 1048576 | tf_op jit(solution)/shard_map/all_to_all | solution.py:153
  15.3 0.7 copy-start.9
  15.3 0.7 copy-start.11
  16.1 8.4 %collective-permute-start.5 = (bf16[1,128,256]{2,1,0:T(8,128)(2,1)S(1)}, bf16[1,128,256]{2,1,0:T(8,128)(2,1)S(1)}, u32[]{:S(2)}, u32[]{:S(2)}) collective-permute-start(bf16[1,128,256]{2,1,0:T(8,128)(2,1)S(1)} %get-tuple-element.60), channel_id=1, source_target_pairs={{0,6},{1,7},{2,0},{3,1},{4,2},{5,3},{6,4},{7,5},{8,14},{9,15},{10,... | collective-permute-start | bytes 196616 | tf_op jit(solution)/shard_map/ppermute | solution.py:145
  19.1 5.4 %collective-permute-start.6 = (bf16[1,128,256]{2,1,0:T(8,128)(2,1)S(1)}, bf16[1,128,256]{2,1,0:T(8,128)(2,1)S(1)}, u32[]{:S(2)}, u32[]{:S(2)}) collective-permute-start(bf16[1,128,256]{2,1,0:T(8,128)(2,1)S(1)} %get-tuple-element.59), channel_id=1, source_target_pairs={{0,7},{1,0},{2,1},{3,2},{4,3},{5,4},{6,5},{7,6},{8,15},{9,8},{10,9... | collective-permute-start | bytes 196616 | tf_op jit(solution)/shard_map/ppermute | solution.py:145
  25.7 27.3 %all-to-all-start.3 = ((bf16[8,64,256]{2,1,0:T(8,128)(2,1)}), bf16[8,64,256]{2,1,0:T(8,128)(2,1)S(1)}, u32[]{:S(2)}, u32[]{:S(2)}) async-start(bf16[8,64,256]{2,1,0:T(8,128)(2,1)} %bitcast.54), calls=%async_computation.3 | async-start | bytes 524288 | tf_op jit(solution)/shard_map/all_to_all | solution.py:130
  45.5 27.5 %collective-permute-start.8 = (bf16[2,4,512,128]{3,2,1,0:T(8,128)(2,1)}, bf16[2,4,512,128]{3,2,1,0:T(8,128)(2,1)S(1)}, u32[]{:S(2)}, u32[]{:S(2)}) collective-permute-start(bf16[2,4,512,128]{3,2,1,0:T(8,128)(2,1)} %get-tuple-element.54), channel_id=1, source_target_pairs={{8,0},{16,8},{24,16},{0,24},{9,1},{17,9},{25,17},{1,25},{10,2},{18... | collective-permute-start | bytes 3145736 | tf_op jit(solution)/shard_map/ppermute | solution.py:43
  49.1 46.7 %collective-permute-start.7 = (bf16[2,4,512,128]{3,2,1,0:T(8,128)(2,1)}, bf16[2,4,512,128]{3,2,1,0:T(8,128)(2,1)}, u32[]{:S(2)}, u32[]{:S(2)}) collective-permute-start(bf16[2,4,512,128]{3,2,1,0:T(8,128)(2,1)} %get-tuple-element.53), channel_id=1, source_target_pairs={{0,8},{8,16},{16,24},{24,0},{1,9},{9,17},{17,25},{25,1},{2,10},{10... | collective-permute-start | bytes 3145736 | tf_op jit(solution)/shard_map/ppermute | solution.py:41
  53.0 11.2 %all-to-all-start.1 = ((bf16[8,64,256]{2,1,0:T(8,128)(2,1)}), bf16[8,64,256]{2,1,0:T(8,128)(2,1)S(1)}, u32[]{:S(2)}, u32[]{:S(2)}) async-start(bf16[8,64,256]{2,1,0:T(8,128)(2,1)} %bitcast.42), calls=%async_computation.1 | async-start | bytes 524288 | tf_op jit(solution)/shard_map/all_to_all | solution.py:129
  73.8 26.4 %copy-start.5 = (bf16[2,4,1024,64]{2,3,1,0:T(8,128)(2,1)S(1)}, bf16[2,4,1024,64]{2,3,1,0:T(8,128)(2,1)}, u32[]{:S(2)}) copy-start(bf16[2,4,1024,64]{2,3,1,0:T(8,128)(2,1)} %get-tuple-element.55) | copy-start | bytes 3145732
  106.6 3.1 copy-start.4
  124.8 2.2 copy-start.2
  124.8 2.3 copy-start.7
  135.5 2.0 copy-start.3
  263.4 8.6 %copy-start.6 = (bf16[8,4,64,64]{2,3,1,0:T(8,128)(2,1)S(1)}, bf16[8,4,64,64]{2,3,1,0:T(8,128)(2,1)}, u32[]{:S(2)}) copy-start(bf16[8,4,64,64]{2,3,1,0:T(8,128)(2,1)} %get-tuple-element.76) | copy-start | bytes 786436
  268.2 50.6 %collective-permute-start.9 = (f32[2,4,512,128]{3,2,1,0:T(8,128)}, f32[2,4,512,128]{3,2,1,0:T(8,128)}, u32[]{:S(2)}, u32[]{:S(2)}) collective-permute-start(f32[2,4,512,128]{3,2,1,0:T(8,128)} %get-tuple-element.37), channel_id=1, source_target_pairs={{0,8},{8,16},{16,24},{24,0},{1,9},{9,17},{17,25},{25,1},{2,10},{10... | collective-permute-start | bytes 6291464 | tf_op jit(solution)/shard_map/ppermute | solution.py:41
  269.6 92.1 %collective-permute-start.10 = (f32[2,4,512,128]{3,2,1,0:T(8,128)}, f32[2,4,512,128]{3,2,1,0:T(8,128)}, u32[]{:S(2)}, u32[]{:S(2)}) collective-permute-start(f32[2,4,512,128]{3,2,1,0:T(8,128)} %get-tuple-element.36), channel_id=1, source_target_pairs={{8,0},{16,8},{24,16},{0,24},{9,1},{17,9},{25,17},{1,25},{10,2},{18... | collective-permute-start | bytes 6291464 | tf_op jit(solution)/shard_map/ppermute | solution.py:43
  273.0 103.9 %all-to-all-start.2 = ((bf16[8,64,256]{2,1,0:T(8,128)(2,1)}), bf16[8,64,256]{2,1,0:T(8,128)(2,1)S(1)}, u32[]{:S(2)}, u32[]{:S(2)}) async-start(bf16[8,64,256]{2,1,0:T(8,128)(2,1)} %copy.188), calls=%async_computation.2 | async-start | bytes 524288 | tf_op jit(solution)/shard_map/all_to_all | solution.py:250
  366.0 3.8 copy-start.12
  369.9 3.5 copy-start.10
  376.8 10.4 %all-to-all-start.4 = ((bf16[8,64,256]{2,1,0:T(8,128)(2,1)}), bf16[8,64,256]{2,1,0:T(8,128)(2,1)S(1)}, u32[]{:S(2)}, u32[]{:S(2)}) async-start(bf16[8,64,256]{2,1,0:T(8,128)(2,1)} %reshape.482), calls=%async_computation.4 | async-start | bytes 524288 | tf_op jit(solution)/shard_map/all_to_all | solution.py:251
  387.2 30.2 %all-to-all-start.5 = ((f32[2,8,128,256]{2,3,0,1:T(8,128)}), f32[2,8,128,256]{2,3,0,1:T(8,128)S(1)}, u32[]{:S(2)}, u32[]{:S(2)}) async-start(f32[2,8,128,256]{2,3,0,1:T(8,128)} %copy.212), calls=%async_computation.5 | async-start | bytes 4194304 | tf_op jit(solution)/shard_map/all_to_all | solution.py:238
  391.1 28.8 %copy-start.1 = (s32[1,8,8]{2,1,0:T(8,128)S(1)}, s32[1,8,8]{2,1,0:T(8,128)}, u32[]{:S(2)}) copy-start(s32[1,8,8]{2,1,0:T(8,128)} %param.11) | copy-start | bytes 772
